TPU v7x, 512 devices: a whole 4x8x8 slice. The times are simulated.
512 devices in a mesh: ctx: 128 (over y, z, core), head: 4 (over x).
Axes of the slice: x: 4, y: 8, z: 8, core: 2. Of those that a mesh axis runs over, the one named last changes fastest.
Arguments:
- queries: bfloat16 [32768, 2048], P('ctx', 'head'), may hold values from -120 to 120
- keys: bfloat16 [32768, 128], P('ctx'), may hold values from -20 to 20
- values: bfloat16 [32768, 128], P('ctx'), may hold values from -6 to 6
- grad_out: bfloat16 [32768, 2048], P('ctx', 'head'), may hold values from -6 to 6
- doc_of_block: int32 [128], replicated, may hold values from 0 to 31, never falling along the last dimension, each value on 1 to 8 neighbouring positions
- pair_list: int32 [128, 7], P('ctx'), may hold values from 0 to 7, as said below
- knock: int32 [16, 128], P('head'), may hold values 0 or 1
Outputs:
- d_queries: bfloat16 [32768, 2048], P('ctx', 'head')
- d_keys: bfloat16 [32768, 128], P('ctx')
- d_values: bfloat16 [32768, 128], P('ctx')
Inputs may be any that keep to these rules, and one draw needn't show every extreme that they name: `pair_list`: row b holds distinct offsets from 1 to 7 in its first entries and 0 in the rest; some row holds all 7 offsets; an offset that reaches before block 0 names no block. `doc_of_block`: never falls along the blocks; each document covers 1 to 8 whole blocks, one exactly 8.
All inputs are finite; a program needn't handle non-finite values. No bound on the sum of `knock` on one device may be relied on, other than what follows from the above.
Results may differ from a plain program's by a relative error of at most 0.01.
Values may be sent and summed in bfloat16 or wider, within the bound.
No kernel may reach another device: no remote copies, remote signals or barrier semaphores. Data moves between devices by JAX's collectives and lax.ppermute only.
A program may use at most 128 MiB of HBM per device.

v0:
```python
import jax
import jax.numpy as jnp
from jax import lax
from jax.sharding import PartitionSpec as P

NEG = -1e30


def from_behind(array, axis, by):
    size = lax.axis_size(axis)
    pairs = [(i, i + by) for i in range(size) if 0 <= i + by < size]
    return lax.ppermute(array, axis, pairs)


def local(queries, keys, values, grad_out, doc_of_block, pair_list, knock):
    rows = keys.shape[0]
    width = keys.shape[1]
    local_heads = queries.shape[1] // width
    reach = pair_list.shape[1] + 1
    blocks = doc_of_block.shape[0]
    scale = width ** (-0.5)
    here = lax.axis_index("ctx")
    query_heads = queries.reshape(rows, local_heads, width)
    grad_heads = grad_out.reshape(rows, local_heads, width)
    packed = jnp.concatenate([keys, values], axis=1)
    lower = jnp.arange(rows)[:, None] >= jnp.arange(rows)[None, :]
    own_doc = lax.dynamic_index_in_dim(doc_of_block, here, 0, keepdims=False)

    def tile_mask(offset):
        if offset == 0:
            return jnp.broadcast_to(lower[None], (local_heads, rows, rows))
        source = here - offset
        clipped = jnp.clip(source, 0, blocks - 1)
        listed = jnp.any(pair_list[0] == offset)
        same_doc = lax.dynamic_index_in_dim(doc_of_block, clipped, 0, keepdims=False) == own_doc
        keeping = lax.dynamic_index_in_dim(knock, clipped, 1, keepdims=False) == 1
        allowed = (source >= 0) & listed & same_doc & keeping
        return jnp.broadcast_to(allowed[:, None, None], (local_heads, rows, rows))

    tiles = [packed]
    current = packed
    for offset in range(1, reach):
        current = from_behind(current, "ctx", 1)
        tiles.append(current)
    top = jnp.full((local_heads, rows, 1), NEG, jnp.float32)
    total = jnp.zeros((local_heads, rows, 1), jnp.float32)
    weighted = jnp.zeros((local_heads, rows, 1), jnp.float32)
    kept = []
    masks = []
    for offset in range(reach):
        mask = tile_mask(offset)
        masks.append(mask)
        first_tile = tiles[offset]
        raw = (
            jnp.einsum(
                "ihd,jd->hij",
                query_heads,
                first_tile[:, :width],
                preferred_element_type=jnp.float32,
            )
            * scale
        )
        scores = jnp.where(mask, raw, NEG)
        grad_probs = jnp.einsum(
            "ihd,jd->hij", grad_heads, first_tile[:, width:], preferred_element_type=jnp.float32
        )
        new_top = jnp.maximum(top, jnp.max(scores, axis=2, keepdims=True))
        factor = jnp.exp(top - new_top)
        shifted = jnp.exp(scores - new_top)
        new_total = total * factor + jnp.sum(shifted, axis=2, keepdims=True)
        new_weighted = weighted * factor + jnp.sum(shifted * grad_probs, axis=2, keepdims=True)
        scores, grad_probs, top, total, weighted = (
            scores,
            grad_probs,
            new_top,
            new_total,
            new_weighted,
        )
        kept.append((scores, grad_probs))
    log_total = top + jnp.log(total)
    delta = weighted / total

    def grad_step(tile, scores, grad_probs, query_sum):
        probs = jnp.exp(scores - log_total)
        grad_scores = probs * (grad_probs - delta)
        probs_low = probs.astype(jnp.bfloat16)
        grad_low = grad_scores.astype(jnp.bfloat16)
        query_add = jnp.einsum(
            "hij,jd->ihd", grad_low, tile[:, :width], preferred_element_type=jnp.float32
        )
        key_part = (
            jnp.einsum("hij,ihd->jd", grad_low, query_heads, preferred_element_type=jnp.float32)
            * scale
        )
        value_part = jnp.einsum(
            "hij,ihd->jd", probs_low, grad_heads, preferred_element_type=jnp.float32
        )
        return (query_sum + query_add, jnp.concatenate([key_part, value_part], axis=1))

    def grad_tile(offset, query_sum):
        scores, grad_probs = kept[offset]
        return grad_step(tiles[offset], scores, grad_probs, query_sum)

    query_sum = jnp.zeros((rows, local_heads, width), jnp.float32)
    carried = None
    for offset in reversed(range(reach)):
        query_sum, term = grad_tile(offset, query_sum)
        if carried is None:
            carried = term
        else:
            carried = (
                from_behind(carried.astype(jnp.bfloat16), "ctx", -1).astype(carried.dtype) + term
            )
    result = lax.psum(carried, "head").astype(jnp.bfloat16)
    d_queries = (query_sum * scale).reshape(rows, local_heads * width).astype(jnp.bfloat16)
    return (d_queries, result[:, :width], result[:, width:])


def solution(mesh):
    in_specs = (
        P("ctx", "head"),
        P("ctx", None),
        P("ctx", None),
        P("ctx", "head"),
        P(),
        P("ctx", None),
        P("head", None),
    )
    out_specs = (P("ctx", "head"), P("ctx", None), P("ctx", None))
    return jax.shard_map(local, mesh=mesh, in_specs=in_specs, out_specs=out_specs, check_vma=False)
```

profile of v0, /device:TPU:32, one launch (start us, length us, event | category | flops | bytes accessed | tf_op | source)
XLA Modules:
  0.0 178.6 jit_solution(8060086629659866876)
XLA Ops:
  0.6 0.9 pad_maximum_fusion
  1.6 1.9 %collective-permute-start = (bf16[256,256]{1,0:T(8,128)(2,1)S(1)}, bf16[256,256]{1,0:T(8,128)(2,1)S(1)}, u32[]{:S(2)}, u32[]{:S(2)}) collective-permute-start(bf16[256,256]{1,0:T(8,128)(2,1)S(1)} %pad_maximum_fusion), channel_id=1, source_target_pairs={{0,4},{4,8},{8,12},{12,16},{16,20},{20,24},{24,28},{28,32},{32,36}... | collective-permute-start | bytes 393224 | tf_op jit(solution)/shard_map/ppermute | solution.py:12
  3.6 0.6 copy-done.17
  4.2 0.7 fusion.100
  13.2 0.8 compare_reduce_fusion
  14.2 0.8 copy-done.14
  20.2 4.4 %collective-permute-start.1 = (bf16[256,256]{1,0:T(8,128)(2,1)S(1)}, bf16[256,256]{1,0:T(8,128)(2,1)S(1)}, u32[]{:S(2)}, u32[]{:S(2)}) collective-permute-start(bf16[256,256]{1,0:T(8,128)(2,1)S(1)} %collective-permute-done), channel_id=1, source_target_pairs={{0,4},{4,8},{8,12},{12,16},{16,20},{20,24},{24,28},{28,32},{32,36}... | collective-permute-start | bytes 393224 | tf_op jit(solution)/shard_map/ppermute | solution.py:12
  24.9 8.2 %collective-permute-done.1 = bf16[256,256]{1,0:T(8,128)(2,1)S(1)} collective-permute-done((bf16[256,256]{1,0:T(8,128)(2,1)S(1)}, bf16[256,256]{1,0:T(8,128)(2,1)S(1)}, u32[]{:S(2)}, u32[]{:S(2)}) %collective-permute-start.1) | collective-permute-done | bytes 131104 | tf_op jit(solution)/shard_map/ppermute | solution.py:12
  33.2 1.9 %collective-permute-start.2 = (bf16[256,256]{1,0:T(8,128)(2,1)S(1)}, bf16[256,256]{1,0:T(8,128)(2,1)S(1)}, u32[]{:S(2)}, u32[]{:S(2)}) collective-permute-start(bf16[256,256]{1,0:T(8,128)(2,1)S(1)} %collective-permute-done.1), channel_id=1, source_target_pairs={{0,4},{4,8},{8,12},{12,16},{16,20},{20,24},{24,28},{28,32},{32,36}... | collective-permute-start | bytes 393224 | tf_op jit(solution)/shard_map/ppermute | solution.py:12
  35.4 7.4 %collective-permute-done.2 = bf16[256,256]{1,0:T(8,128)(2,1)S(1)} collective-permute-done((bf16[256,256]{1,0:T(8,128)(2,1)S(1)}, bf16[256,256]{1,0:T(8,128)(2,1)S(1)}, u32[]{:S(2)}, u32[]{:S(2)}) %collective-permute-start.2) | collective-permute-done | bytes 131104 | tf_op jit(solution)/shard_map/ppermute | solution.py:12
  42.8 1.9 %collective-permute-start.3 = (bf16[256,256]{1,0:T(8,128)(2,1)S(1)}, bf16[256,256]{1,0:T(8,128)(2,1)S(1)}, u32[]{:S(2)}, u32[]{:S(2)}) collective-permute-start(bf16[256,256]{1,0:T(8,128)(2,1)S(1)} %collective-permute-done.2), channel_id=1, source_target_pairs={{0,4},{4,8},{8,12},{12,16},{16,20},{20,24},{24,28},{28,32},{32,36}... | collective-permute-start | bytes 393224 | tf_op jit(solution)/shard_map/ppermute | solution.py:12
  45.0 7.4 %collective-permute-done.3 = bf16[256,256]{1,0:T(8,128)(2,1)S(1)} collective-permute-done((bf16[256,256]{1,0:T(8,128)(2,1)S(1)}, bf16[256,256]{1,0:T(8,128)(2,1)S(1)}, u32[]{:S(2)}, u32[]{:S(2)}) %collective-permute-start.3) | collective-permute-done | bytes 131104 | tf_op jit(solution)/shard_map/ppermute | solution.py:12
  52.3 1.9 %collective-permute-start.4 = (bf16[256,256]{1,0:T(8,128)(2,1)S(1)}, bf16[256,256]{1,0:T(8,128)(2,1)S(1)}, u32[]{:S(2)}, u32[]{:S(2)}) collective-permute-start(bf16[256,256]{1,0:T(8,128)(2,1)S(1)} %collective-permute-done.3), channel_id=1, source_target_pairs={{0,4},{4,8},{8,12},{12,16},{16,20},{20,24},{24,28},{28,32},{32,36}... | collective-permute-start | bytes 393224 | tf_op jit(solution)/shard_map/ppermute | solution.py:12
  54.6 7.4 %collective-permute-done.4 = bf16[256,256]{1,0:T(8,128)(2,1)S(1)} collective-permute-done((bf16[256,256]{1,0:T(8,128)(2,1)S(1)}, bf16[256,256]{1,0:T(8,128)(2,1)S(1)}, u32[]{:S(2)}, u32[]{:S(2)}) %collective-permute-start.4) | collective-permute-done | bytes 131104 | tf_op jit(solution)/shard_map/ppermute | solution.py:12
  61.9 1.9 %collective-permute-start.5 = (bf16[256,256]{1,0:T(8,128)(2,1)S(1)}, bf16[256,256]{1,0:T(8,128)(2,1)S(1)}, u32[]{:S(2)}, u32[]{:S(2)}) collective-permute-start(bf16[256,256]{1,0:T(8,128)(2,1)S(1)} %collective-permute-done.4), channel_id=1, source_target_pairs={{0,4},{4,8},{8,12},{12,16},{16,20},{20,24},{24,28},{28,32},{32,36}... | collective-permute-start | bytes 393224 | tf_op jit(solution)/shard_map/ppermute | solution.py:12
  64.2 7.4 %collective-permute-done.5 = bf16[256,256]{1,0:T(8,128)(2,1)S(1)} collective-permute-done((bf16[256,256]{1,0:T(8,128)(2,1)S(1)}, bf16[256,256]{1,0:T(8,128)(2,1)S(1)}, u32[]{:S(2)}, u32[]{:S(2)}) %collective-permute-start.5) | collective-permute-done | bytes 131104 | tf_op jit(solution)/shard_map/ppermute | solution.py:12
  71.5 1.9 %collective-permute-start.6 = (bf16[256,256]{1,0:T(8,128)(2,1)S(1)}, bf16[256,256]{1,0:T(8,128)(2,1)S(1)}, u32[]{:S(2)}, u32[]{:S(2)}) collective-permute-start(bf16[256,256]{1,0:T(8,128)(2,1)S(1)} %collective-permute-done.5), channel_id=1, source_target_pairs={{0,4},{4,8},{8,12},{12,16},{16,20},{20,24},{24,28},{28,32},{32,36}... | collective-permute-start | bytes 393224 | tf_op jit(solution)/shard_map/ppermute | solution.py:12
  73.8 7.4 %collective-permute-done.6 = bf16[256,256]{1,0:T(8,128)(2,1)S(1)} collective-permute-done((bf16[256,256]{1,0:T(8,128)(2,1)S(1)}, bf16[256,256]{1,0:T(8,128)(2,1)S(1)}, u32[]{:S(2)}, u32[]{:S(2)}) %collective-permute-start.6) | collective-permute-done | bytes 131104 | tf_op jit(solution)/shard_map/ppermute | solution.py:12
  81.5 0.8 copy-done.15
  84.9 0.3 fusion.34
  85.3 1.9 %multiply_convert_fusion.7 = (bf16[4,256,256]{1,2,0:T(8,128)(2,1)S(1)}, bf16[4,256,256]{1,2,0:T(8,128)(2,1)S(1)}, bf16[4,256,256]{1,2,0:T(8,128)(2,1)S(1)}, bf16...) fusion(f32[4,256,256]{1,2,0:T(8,128)S(1)} %get-tuple-element.80, ...), kind=kLoop, calls=%fused_computation.83 | loop fusion | flops 8388608 | bytes 20979712 | tf_op jit(solution)/shard_map/convert_element_type | solution.py:87
  88.1 1.0 fusion.26
  91.9 0.6 copy-done.12
  92.8 0.4 fusion.24
  93.2 0.8 copy.74
  94.1 2.1 %collective-permute-start.7 = (bf16[256,256]{0,1:T(8,128)(2,1)S(1)}, bf16[256,256]{0,1:T(8,128)(2,1)S(1)}, u32[]{:S(2)}, u32[]{:S(2)}) collective-permute-start(bf16[256,256]{0,1:T(8,128)(2,1)S(1)} %pad_maximum_fusion.1), channel_id=1, source_target_pairs={{4,0},{8,4},{12,8},{16,12},{20,16},{24,20},{28,24},{32,28},{36,32}... | collective-permute-start | bytes 393224 | tf_op jit(solution)/shard_map/ppermute | solution.py:12
  96.1 1.5 convolution_bitcast_fusion.21
  97.7 0.9 collective-permute-done.7
  98.7 7.2 %collective-permute-start.8 = (bf16[256,256]{0,1:T(8,128)(2,1)S(1)}, bf16[256,256]{0,1:T(8,128)(2,1)S(1)}, u32[]{:S(2)}, u32[]{:S(2)}) collective-permute-start(bf16[256,256]{0,1:T(8,128)(2,1)S(1)} %fusion.67), channel_id=1, source_target_pairs={{4,0},{8,4},{12,8},{16,12},{20,16},{24,20},{28,24},{32,28},{36,32}... | collective-permute-start | bytes 393224 | tf_op jit(solution)/shard_map/ppermute | solution.py:12
  105.9 0.3 convolution_bitcast_fusion.19
  106.3 2.2 %collective-permute-done.8 = bf16[256,256]{0,1:T(8,128)(2,1)S(1)} collective-permute-done((bf16[256,256]{0,1:T(8,128)(2,1)S(1)}, bf16[256,256]{0,1:T(8,128)(2,1)S(1)}, u32[]{:S(2)}, u32[]{:S(2)}) %collective-permute-start.8) | collective-permute-done | bytes 131104 | tf_op jit(solution)/shard_map/ppermute | solution.py:12
  108.5 7.2 %collective-permute-start.9 = (bf16[256,256]{0,1:T(8,128)(2,1)S(1)}, bf16[256,256]{0,1:T(8,128)(2,1)S(1)}, u32[]{:S(2)}, u32[]{:S(2)}) collective-permute-start(bf16[256,256]{0,1:T(8,128)(2,1)S(1)} %fusion.68), channel_id=1, source_target_pairs={{4,0},{8,4},{12,8},{16,12},{20,16},{24,20},{28,24},{32,28},{36,32}... | collective-permute-start | bytes 393224 | tf_op jit(solution)/shard_map/ppermute | solution.py:12
  115.7 0.3 convolution_bitcast_fusion.17
  116.1 2.2 %collective-permute-done.9 = bf16[256,256]{0,1:T(8,128)(2,1)S(1)} collective-permute-done((bf16[256,256]{0,1:T(8,128)(2,1)S(1)}, bf16[256,256]{0,1:T(8,128)(2,1)S(1)}, u32[]{:S(2)}, u32[]{:S(2)}) %collective-permute-start.9) | collective-permute-done | bytes 131104 | tf_op jit(solution)/shard_map/ppermute | solution.py:12
  118.3 7.2 %collective-permute-start.10 = (bf16[256,256]{0,1:T(8,128)(2,1)S(1)}, bf16[256,256]{0,1:T(8,128)(2,1)S(1)}, u32[]{:S(2)}, u32[]{:S(2)}) collective-permute-start(bf16[256,256]{0,1:T(8,128)(2,1)S(1)} %fusion.69), channel_id=1, source_target_pairs={{4,0},{8,4},{12,8},{16,12},{20,16},{24,20},{28,24},{32,28},{36,32}... | collective-permute-start | bytes 393224 | tf_op jit(solution)/shard_map/ppermute | solution.py:12
  125.5 0.3 convolution_bitcast_fusion.15
  125.8 2.2 %collective-permute-done.10 = bf16[256,256]{0,1:T(8,128)(2,1)S(1)} collective-permute-done((bf16[256,256]{0,1:T(8,128)(2,1)S(1)}, bf16[256,256]{0,1:T(8,128)(2,1)S(1)}, u32[]{:S(2)}, u32[]{:S(2)}) %collective-permute-start.10) | collective-permute-done | bytes 131104 | tf_op jit(solution)/shard_map/ppermute | solution.py:12
  128.0 7.1 %collective-permute-start.11 = (bf16[256,256]{0,1:T(8,128)(2,1)S(1)}, bf16[256,256]{0,1:T(8,128)(2,1)S(1)}, u32[]{:S(2)}, u32[]{:S(2)}) collective-permute-start(bf16[256,256]{0,1:T(8,128)(2,1)S(1)} %fusion.70), channel_id=1, source_target_pairs={{4,0},{8,4},{12,8},{16,12},{20,16},{24,20},{28,24},{32,28},{36,32}... | collective-permute-start | bytes 393224 | tf_op jit(solution)/shard_map/ppermute | solution.py:12
  135.1 0.3 convolution_bitcast_fusion.13
  135.5 2.2 %collective-permute-done.11 = bf16[256,256]{0,1:T(8,128)(2,1)S(1)} collective-permute-done((bf16[256,256]{0,1:T(8,128)(2,1)S(1)}, bf16[256,256]{0,1:T(8,128)(2,1)S(1)}, u32[]{:S(2)}, u32[]{:S(2)}) %collective-permute-start.11) | collective-permute-done | bytes 131104 | tf_op jit(solution)/shard_map/ppermute | solution.py:12
  137.7 7.1 %collective-permute-start.12 = (bf16[256,256]{0,1:T(8,128)(2,1)S(1)}, bf16[256,256]{0,1:T(8,128)(2,1)S(1)}, u32[]{:S(2)}, u32[]{:S(2)}) collective-permute-start(bf16[256,256]{0,1:T(8,128)(2,1)S(1)} %fusion.71), channel_id=1, source_target_pairs={{4,0},{8,4},{12,8},{16,12},{20,16},{24,20},{28,24},{32,28},{36,32}... | collective-permute-start | bytes 393224 | tf_op jit(solution)/shard_map/ppermute | solution.py:12
  145.1 2.2 %collective-permute-done.12 = bf16[256,256]{0,1:T(8,128)(2,1)S(1)} collective-permute-done((bf16[256,256]{0,1:T(8,128)(2,1)S(1)}, bf16[256,256]{0,1:T(8,128)(2,1)S(1)}, u32[]{:S(2)}, u32[]{:S(2)}) %collective-permute-start.12) | collective-permute-done | bytes 131104 | tf_op jit(solution)/shard_map/ppermute | solution.py:12
  147.3 7.1 %collective-permute-start.13 = (bf16[256,256]{0,1:T(8,128)(2,1)S(1)}, bf16[256,256]{0,1:T(8,128)(2,1)S(1)}, u32[]{:S(2)}, u32[]{:S(2)}) collective-permute-start(bf16[256,256]{0,1:T(8,128)(2,1)S(1)} %fusion.72), channel_id=1, source_target_pairs={{4,0},{8,4},{12,8},{16,12},{20,16},{24,20},{28,24},{32,28},{36,32}... | collective-permute-start | bytes 393224 | tf_op jit(solution)/shard_map/ppermute | solution.py:12
  154.4 0.3 convolution_bitcast_fusion.9
  154.7 2.2 %collective-permute-done.13 = bf16[256,256]{0,1:T(8,128)(2,1)S(1)} collective-permute-done((bf16[256,256]{0,1:T(8,128)(2,1)S(1)}, bf16[256,256]{0,1:T(8,128)(2,1)S(1)}, u32[]{:S(2)}, u32[]{:S(2)}) %collective-permute-start.13) | collective-permute-done | bytes 131104 | tf_op jit(solution)/shard_map/ppermute | solution.py:12
  156.9 20.2 %all-reduce.1 = bf16[256,256]{0,1:T(8,128)(2,1)S(1)} all-reduce(f32[256,256]{0,1:T(8,128)S(1)} %maximum_add_fusion.6), channel_id=1, replica_groups=mesh['ctx'=128,'head'=4] {'head'}, use_global_device_ids=true, to_apply=%region_31.32 | all-reduce | flops 65536 | bytes 393216 | tf_op jit(solution)/shard_map/psum | solution.py:114
  177.1 0.7 copy.76
  177.9 0.7 copy.75
  (82 shorter events, 10.2 us)
Async XLA Ops:
  0.6 13.4 %copy-start.13 = (bf16[256,512]{1,0:T(8,128)(2,1)S(1)}, bf16[256,512]{1,0:T(8,128)(2,1)}, u32[]{:S(2)}) copy-start(bf16[256,512]{1,0:T(8,128)(2,1)} %param.7) | copy-start | bytes 786436
  1.6 18.6 %collective-permute-start = (bf16[256,256]{1,0:T(8,128)(2,1)S(1)}, bf16[256,256]{1,0:T(8,128)(2,1)S(1)}, u32[]{:S(2)}, u32[]{:S(2)}) collective-permute-start(bf16[256,256]{1,0:T(8,128)(2,1)S(1)} %pad_maximum_fusion), channel_id=1, source_target_pairs={{0,4},{4,8},{8,12},{12,16},{16,20},{20,24},{24,28},{28,32},{32,36}... | collective-permute-start | bytes 393224 | tf_op jit(solution)/shard_map/ppermute | solution.py:12
  3.6 0.7 copy-start.17
  12.0 1.2 copy-start.18
  14.0 1.0 copy-start.14
  15.0 4.6 %copy-start.16 = (s32[4,128]{1,0:T(4,128)S(1)}, s32[4,128]{1,0:T(4,128)}, u32[]{:S(2)}) copy-start(s32[4,128]{1,0:T(4,128)} %param.13) | copy-start | bytes 6148
  15.1 4.8 %copy-start.9 = (bf16[256,128]{1,0:T(8,128)(2,1)S(1)}, bf16[256,128]{1,0:T(8,128)(2,1)}, u32[]{:S(2)}) copy-start(bf16[256,128]{1,0:T(8,128)(2,1)} %param.8) | copy-start | bytes 196612
  20.2 64.3 %copy-start.11 = (bf16[256,256]{1,0:T(8,128)(2,1)}, bf16[256,256]{1,0:T(8,128)(2,1)S(1)}, u32[]{:S(2)}) copy-start(bf16[256,256]{1,0:T(8,128)(2,1)S(1)} %collective-permute-done) | copy-start | bytes 393220
  20.2 12.9 %collective-permute-start.1 = (bf16[256,256]{1,0:T(8,128)(2,1)S(1)}, bf16[256,256]{1,0:T(8,128)(2,1)S(1)}, u32[]{:S(2)}, u32[]{:S(2)}) collective-permute-start(bf16[256,256]{1,0:T(8,128)(2,1)S(1)} %collective-permute-done), channel_id=1, source_target_pairs={{0,4},{4,8},{8,12},{12,16},{16,20},{20,24},{24,28},{28,32},{32,36}... | collective-permute-start | bytes 393224 | tf_op jit(solution)/shard_map/ppermute | solution.py:12
  33.2 9.6 %collective-permute-start.2 = (bf16[256,256]{1,0:T(8,128)(2,1)S(1)}, bf16[256,256]{1,0:T(8,128)(2,1)S(1)}, u32[]{:S(2)}, u32[]{:S(2)}) collective-permute-start(bf16[256,256]{1,0:T(8,128)(2,1)S(1)} %collective-permute-done.1), channel_id=1, source_target_pairs={{0,4},{4,8},{8,12},{12,16},{16,20},{20,24},{24,28},{28,32},{32,36}... | collective-permute-start | bytes 393224 | tf_op jit(solution)/shard_map/ppermute | solution.py:12
  35.4 49.9 %copy-start = (f32[4,256,256]{1,2,0:T(8,128)}, f32[4,256,256]{1,2,0:T(8,128)S(1)}, u32[]{:S(2)}) copy-start(f32[4,256,256]{1,2,0:T(8,128)S(1)} %get-tuple-element.75) | copy-start | bytes 3145732
  42.8 9.6 %collective-permute-start.3 = (bf16[256,256]{1,0:T(8,128)(2,1)S(1)}, bf16[256,256]{1,0:T(8,128)(2,1)S(1)}, u32[]{:S(2)}, u32[]{:S(2)}) collective-permute-start(bf16[256,256]{1,0:T(8,128)(2,1)S(1)} %collective-permute-done.2), channel_id=1, source_target_pairs={{0,4},{4,8},{8,12},{12,16},{16,20},{20,24},{24,28},{28,32},{32,36}... | collective-permute-start | bytes 393224 | tf_op jit(solution)/shard_map/ppermute | solution.py:12
  45.0 40.3 %copy-start.2 = (f32[4,256,256]{1,2,0:T(8,128)}, f32[4,256,256]{1,2,0:T(8,128)S(1)}, u32[]{:S(2)}) copy-start(f32[4,256,256]{1,2,0:T(8,128)S(1)} %get-tuple-element.73) | copy-start | bytes 3145732
  52.3 9.6 %collective-permute-start.4 = (bf16[256,256]{1,0:T(8,128)(2,1)S(1)}, bf16[256,256]{1,0:T(8,128)(2,1)S(1)}, u32[]{:S(2)}, u32[]{:S(2)}) collective-permute-start(bf16[256,256]{1,0:T(8,128)(2,1)S(1)} %collective-permute-done.3), channel_id=1, source_target_pairs={{0,4},{4,8},{8,12},{12,16},{16,20},{20,24},{24,28},{28,32},{32,36}... | collective-permute-start | bytes 393224 | tf_op jit(solution)/shard_map/ppermute | solution.py:12
  54.6 30.7 %copy-start.4 = (f32[4,256,256]{1,2,0:T(8,128)}, f32[4,256,256]{1,2,0:T(8,128)S(1)}, u32[]{:S(2)}) copy-start(f32[4,256,256]{1,2,0:T(8,128)S(1)} %get-tuple-element.71) | copy-start | bytes 3145732
  61.9 9.6 %collective-permute-start.5 = (bf16[256,256]{1,0:T(8,128)(2,1)S(1)}, bf16[256,256]{1,0:T(8,128)(2,1)S(1)}, u32[]{:S(2)}, u32[]{:S(2)}) collective-permute-start(bf16[256,256]{1,0:T(8,128)(2,1)S(1)} %collective-permute-done.4), channel_id=1, source_target_pairs={{0,4},{4,8},{8,12},{12,16},{16,20},{20,24},{24,28},{28,32},{32,36}... | collective-permute-start | bytes 393224 | tf_op jit(solution)/shard_map/ppermute | solution.py:12
  64.2 21.1 %copy-start.6 = (f32[4,256,256]{1,2,0:T(8,128)}, f32[4,256,256]{1,2,0:T(8,128)S(1)}, u32[]{:S(2)}) copy-start(f32[4,256,256]{1,2,0:T(8,128)S(1)} %get-tuple-element.69) | copy-start | bytes 3145732
  71.5 9.6 %collective-permute-start.6 = (bf16[256,256]{1,0:T(8,128)(2,1)S(1)}, bf16[256,256]{1,0:T(8,128)(2,1)S(1)}, u32[]{:S(2)}, u32[]{:S(2)}) collective-permute-start(bf16[256,256]{1,0:T(8,128)(2,1)S(1)} %collective-permute-done.5), channel_id=1, source_target_pairs={{0,4},{4,8},{8,12},{12,16},{16,20},{20,24},{24,28},{28,32},{32,36}... | collective-permute-start | bytes 393224 | tf_op jit(solution)/shard_map/ppermute | solution.py:12
  73.8 11.6 %copy-start.8 = (f32[4,256,256]{1,2,0:T(8,128)}, f32[4,256,256]{1,2,0:T(8,128)S(1)}, u32[]{:S(2)}) copy-start(f32[4,256,256]{1,2,0:T(8,128)S(1)} %get-tuple-element.67) | copy-start | bytes 3145732
  81.4 0.8 copy-start.15
  91.7 0.9 copy-start.12
  94.1 4.6 %copy-start.10 = (f32[256,128]{0,1:T(8,128)S(1)}, f32[256,128]{0,1:T(8,128)}, u32[]{:S(2)}) copy-start(f32[256,128]{0,1:T(8,128)} %fusion.26) | copy-start | bytes 393220
  94.1 11.9 %copy-start.7 = (f32[4,256,256]{1,2,0:T(8,128)S(1)}, f32[4,256,256]{1,2,0:T(8,128)}, u32[]{:S(2)}) copy-start(f32[4,256,256]{1,2,0:T(8,128)} %copy-done.6) | copy-start | bytes 3145732
  94.1 4.6 %collective-permute-start.7 = (bf16[256,256]{0,1:T(8,128)(2,1)S(1)}, bf16[256,256]{0,1:T(8,128)(2,1)S(1)}, u32[]{:S(2)}, u32[]{:S(2)}) collective-permute-start(bf16[256,256]{0,1:T(8,128)(2,1)S(1)} %pad_maximum_fusion.1), channel_id=1, source_target_pairs={{4,0},{8,4},{12,8},{16,12},{20,16},{24,20},{28,24},{32,28},{36,32}... | collective-permute-start | bytes 393224 | tf_op jit(solution)/shard_map/ppermute | solution.py:12
  98.7 17.0 %copy-start.5 = (f32[4,256,256]{1,2,0:T(8,128)S(1)}, f32[4,256,256]{1,2,0:T(8,128)}, u32[]{:S(2)}) copy-start(f32[4,256,256]{1,2,0:T(8,128)} %copy-done.4) | copy-start | bytes 3145732
  98.7 9.7 %collective-permute-start.8 = (bf16[256,256]{0,1:T(8,128)(2,1)S(1)}, bf16[256,256]{0,1:T(8,128)(2,1)S(1)}, u32[]{:S(2)}, u32[]{:S(2)}) collective-permute-start(bf16[256,256]{0,1:T(8,128)(2,1)S(1)} %fusion.67), channel_id=1, source_target_pairs={{4,0},{8,4},{12,8},{16,12},{20,16},{24,20},{28,24},{32,28},{36,32}... | collective-permute-start | bytes 393224 | tf_op jit(solution)/shard_map/ppermute | solution.py:12
  108.5 17.0 %copy-start.3 = (f32[4,256,256]{1,2,0:T(8,128)S(1)}, f32[4,256,256]{1,2,0:T(8,128)}, u32[]{:S(2)}) copy-start(f32[4,256,256]{1,2,0:T(8,128)} %copy-done.2) | copy-start | bytes 3145732
  108.5 9.7 %collective-permute-start.9 = (bf16[256,256]{0,1:T(8,128)(2,1)S(1)}, bf16[256,256]{0,1:T(8,128)(2,1)S(1)}, u32[]{:S(2)}, u32[]{:S(2)}) collective-permute-start(bf16[256,256]{0,1:T(8,128)(2,1)S(1)} %fusion.68), channel_id=1, source_target_pairs={{4,0},{8,4},{12,8},{16,12},{20,16},{24,20},{28,24},{32,28},{36,32}... | collective-permute-start | bytes 393224 | tf_op jit(solution)/shard_map/ppermute | solution.py:12
  118.2 16.9 %copy-start.1 = (f32[4,256,256]{1,2,0:T(8,128)S(1)}, f32[4,256,256]{1,2,0:T(8,128)}, u32[]{:S(2)}) copy-start(f32[4,256,256]{1,2,0:T(8,128)} %copy-done) | copy-start | bytes 3145732
  118.3 9.7 %collective-permute-start.10 = (bf16[256,256]{0,1:T(8,128)(2,1)S(1)}, bf16[256,256]{0,1:T(8,128)(2,1)S(1)}, u32[]{:S(2)}, u32[]{:S(2)}) collective-permute-start(bf16[256,256]{0,1:T(8,128)(2,1)S(1)} %fusion.69), channel_id=1, source_target_pairs={{4,0},{8,4},{12,8},{16,12},{20,16},{24,20},{28,24},{32,28},{36,32}... | collective-permute-start | bytes 393224 | tf_op jit(solution)/shard_map/ppermute | solution.py:12
  128.0 9.6 %collective-permute-start.11 = (bf16[256,256]{0,1:T(8,128)(2,1)S(1)}, bf16[256,256]{0,1:T(8,128)(2,1)S(1)}, u32[]{:S(2)}, u32[]{:S(2)}) collective-permute-start(bf16[256,256]{0,1:T(8,128)(2,1)S(1)} %fusion.70), channel_id=1, source_target_pairs={{4,0},{8,4},{12,8},{16,12},{20,16},{24,20},{28,24},{32,28},{36,32}... | collective-permute-start | bytes 393224 | tf_op jit(solution)/shard_map/ppermute | solution.py:12
  137.7 9.6 %collective-permute-start.12 = (bf16[256,256]{0,1:T(8,128)(2,1)S(1)}, bf16[256,256]{0,1:T(8,128)(2,1)S(1)}, u32[]{:S(2)}, u32[]{:S(2)}) collective-permute-start(bf16[256,256]{0,1:T(8,128)(2,1)S(1)} %fusion.71), channel_id=1, source_target_pairs={{4,0},{8,4},{12,8},{16,12},{20,16},{24,20},{28,24},{32,28},{36,32}... | collective-permute-start | bytes 393224 | tf_op jit(solution)/shard_map/ppermute | solution.py:12
  147.3 9.6 %collective-permute-start.13 = (bf16[256,256]{0,1:T(8,128)(2,1)S(1)}, bf16[256,256]{0,1:T(8,128)(2,1)S(1)}, u32[]{:S(2)}, u32[]{:S(2)}) collective-permute-start(bf16[256,256]{0,1:T(8,128)(2,1)S(1)} %fusion.72), channel_id=1, source_target_pairs={{4,0},{8,4},{12,8},{16,12},{20,16},{24,20},{28,24},{32,28},{36,32}... | collective-permute-start | bytes 393224 | tf_op jit(solution)/shard_map/ppermute | solution.py:12
where the time goes:
time: 179 us
  starting transfers between devices  60.9 us (34%)
  waiting for transfers between devices  58.9 us (33%)
  blocking collectives  20.2 us (11%)
  between operations  14.1 us (8%)
  matrix products  14 us (8%)
  local copies, waits for them, and re-layouts  6.25 us (3%)
  other arithmetic  4.23 us (2%)
    ppermute x14, starting transfers between devices, from_behind(): return lax.ppermute(array, axis, pairs)  60.9 us
    ppermute x14, waiting for transfers between devices, from_behind(): return lax.ppermute(array, axis, pairs)  58.9 us
    psum x1, blocking collectives, local(): result = lax.psum(carried, 'head').astype(jnp.bfloat16)  20.2 us
    unnamed x41, local copies, waits for them, and re-layouts  5.3 us
    dot_general x8, matrix products, grad_step(): jnp.einsum('hij,ihd->jd', probs_low, grad_heads, preferred_element_type=j...  3.82 us
  transfers between devices with their start and end apart: 14, of which 13 were waited for; matrix products, arithmetic and copies ran while one was open for 4% of the time, Pallas kernels for 0%

commit v1 on v0

--- a/solution.py
+++ b/solution.py
@@ -111,7 +111,7 @@
             carried = (
                 from_behind(carried.astype(jnp.bfloat16), "ctx", -1).astype(carried.dtype) + term
             )
-    result = lax.psum(carried, "head").astype(jnp.bfloat16)
+    result = jnp.sum(lax.all_gather(carried, "head"), axis=0).astype(jnp.bfloat16)
     d_queries = (query_sum * scale).reshape(rows, local_heads * width).astype(jnp.bfloat16)
     return (d_queries, result[:, :width], result[:, width:])
 

time: 179 us -> 200 us (1.12)
  the two profiles are of different devices: /device:TPU:32 before, /device:TPU:1 now
where the time goes in v1:
time: 200 us; the launch traced here: 199 us
  waiting for transfers between devices  100 us (50%)
  starting transfers between devices  41.6 us (21%)
  between operations  27.4 us (14%)
  matrix products  14.6 us (7%)
  local copies, waits for them, and re-layouts  9.52 us (5%)
  other arithmetic  5.55 us (3%)
    all_gather x1, waiting for transfers between devices, local(): lax.all_gather(carried, 'head')  61.9 us
    ppermute x14, starting transfers between devices, from_behind(): return lax.ppermute(array, axis, pairs)  41.6 us
    ppermute x14, waiting for transfers between devices, from_behind(): return lax.ppermute(array, axis, pairs)  38.5 us
    unnamed x39, local copies, waits for them, and re-layouts  6.87 us
    dot_general x8, matrix products, grad_step(): jnp.einsum('hij,jd->ihd', grad_low, tile[:, :width], preferred_element_ty...  4.61 us
  transfers between devices with their start and end apart: 15, of which 14 were waited for; matrix products, arithmetic and copies ran while one was open for 5% of the time, Pallas kernels for 0%

profile of v1, /device:TPU:1, one launch (start us, length us, event | category | flops | bytes accessed | tf_op | source)
XLA Modules:
  0.0 199.2 jit_solution(17215448019655879627)
XLA Ops:
  7.2 0.9 pad_maximum_fusion
  8.1 5.4 %collective-permute-start = (bf16[256,256]{1,0:T(8,128)(2,1)S(1)}, bf16[256,256]{1,0:T(8,128)(2,1)S(1)}, u32[]{:S(2)}, u32[]{:S(2)}) collective-permute-start(bf16[256,256]{1,0:T(8,128)(2,1)S(1)} %pad_maximum_fusion), channel_id=1, source_target_pairs={{0,4},{4,8},{8,12},{12,16},{16,20},{20,24},{24,28},{28,32},{32,36}... | collective-permute-start | bytes 393224 | tf_op jit(solution)/shard_map/ppermute | solution.py:12
  13.6 0.6 copy-done.16
  14.3 0.7 fusion.100
  23.3 0.8 compare_reduce_fusion
  24.2 0.8 copy-done.13
  30.3 1.9 collective-permute-start.1
  32.5 2.7 %collective-permute-done.1 = bf16[256,256]{1,0:T(8,128)(2,1)S(1)} collective-permute-done((bf16[256,256]{1,0:T(8,128)(2,1)S(1)}, bf16[256,256]{1,0:T(8,128)(2,1)S(1)}, u32[]{:S(2)}, u32[]{:S(2)}) %collective-permute-start.1) | collective-permute-done | bytes 131104 | tf_op jit(solution)/shard_map/ppermute | solution.py:12
  35.2 3.3 %collective-permute-start.2 = (bf16[256,256]{1,0:T(8,128)(2,1)S(1)}, bf16[256,256]{1,0:T(8,128)(2,1)S(1)}, u32[]{:S(2)}, u32[]{:S(2)}) collective-permute-start(bf16[256,256]{1,0:T(8,128)(2,1)S(1)} %collective-permute-done.1), channel_id=1, source_target_pairs={{0,4},{4,8},{8,12},{12,16},{16,20},{20,24},{24,28},{28,32},{32,36}... | collective-permute-start | bytes 393224 | tf_op jit(solution)/shard_map/ppermute | solution.py:12
  38.8 1.6 collective-permute-done.2
  40.4 4.3 %collective-permute-start.3 = (bf16[256,256]{1,0:T(8,128)(2,1)S(1)}, bf16[256,256]{1,0:T(8,128)(2,1)S(1)}, u32[]{:S(2)}, u32[]{:S(2)}) collective-permute-start(bf16[256,256]{1,0:T(8,128)(2,1)S(1)} %collective-permute-done.2), channel_id=1, source_target_pairs={{0,4},{4,8},{8,12},{12,16},{16,20},{20,24},{24,28},{28,32},{32,36}... | collective-permute-start | bytes 393224 | tf_op jit(solution)/shard_map/ppermute | solution.py:12
  45.1 1.6 collective-permute-done.3
  46.7 4.3 %collective-permute-start.4 = (bf16[256,256]{1,0:T(8,128)(2,1)S(1)}, bf16[256,256]{1,0:T(8,128)(2,1)S(1)}, u32[]{:S(2)}, u32[]{:S(2)}) collective-permute-start(bf16[256,256]{1,0:T(8,128)(2,1)S(1)} %collective-permute-done.3), channel_id=1, source_target_pairs={{0,4},{4,8},{8,12},{12,16},{16,20},{20,24},{24,28},{28,32},{32,36}... | collective-permute-start | bytes 393224 | tf_op jit(solution)/shard_map/ppermute | solution.py:12
  51.3 1.6 collective-permute-done.4
  53.0 4.3 %collective-permute-start.5 = (bf16[256,256]{1,0:T(8,128)(2,1)S(1)}, bf16[256,256]{1,0:T(8,128)(2,1)S(1)}, u32[]{:S(2)}, u32[]{:S(2)}) collective-permute-start(bf16[256,256]{1,0:T(8,128)(2,1)S(1)} %collective-permute-done.4), channel_id=1, source_target_pairs={{0,4},{4,8},{8,12},{12,16},{16,20},{20,24},{24,28},{28,32},{32,36}... | collective-permute-start | bytes 393224 | tf_op jit(solution)/shard_map/ppermute | solution.py:12
  57.6 1.6 collective-permute-done.5
  59.2 4.3 %collective-permute-start.6 = (bf16[256,256]{1,0:T(8,128)(2,1)S(1)}, bf16[256,256]{1,0:T(8,128)(2,1)S(1)}, u32[]{:S(2)}, u32[]{:S(2)}) collective-permute-start(bf16[256,256]{1,0:T(8,128)(2,1)S(1)} %collective-permute-done.5), channel_id=1, source_target_pairs={{0,4},{4,8},{8,12},{12,16},{16,20},{20,24},{24,28},{28,32},{32,36}... | collective-permute-start | bytes 393224 | tf_op jit(solution)/shard_map/ppermute | solution.py:12
  63.9 1.6 collective-permute-done.6
  65.8 0.8 copy-done.14
  69.7 1.8 multiply_convert_fusion.7
  71.9 1.1 convolution_bitcast_fusion.8
  75.2 1.9 collective-permute-start.7
  77.1 1.1 fusion.81
  78.5 3.7 %collective-permute-done.7 = bf16[256,256]{0,1:T(8,128)(2,1)S(1)} collective-permute-done((bf16[256,256]{0,1:T(8,128)(2,1)S(1)}, bf16[256,256]{0,1:T(8,128)(2,1)S(1)}, u32[]{:S(2)}, u32[]{:S(2)}) %collective-permute-start.7) | collective-permute-done | bytes 131104 | tf_op jit(solution)/shard_map/ppermute | solution.py:12
  82.2 1.9 collective-permute-start.8
  84.5 4.0 %collective-permute-done.8 = bf16[256,256]{0,1:T(8,128)(2,1)S(1)} collective-permute-done((bf16[256,256]{0,1:T(8,128)(2,1)S(1)}, bf16[256,256]{0,1:T(8,128)(2,1)S(1)}, u32[]{:S(2)}, u32[]{:S(2)}) %collective-permute-start.8) | collective-permute-done | bytes 131104 | tf_op jit(solution)/shard_map/ppermute | solution.py:12
  88.5 1.9 collective-permute-start.9
  90.8 4.0 %collective-permute-done.9 = bf16[256,256]{0,1:T(8,128)(2,1)S(1)} collective-permute-done((bf16[256,256]{0,1:T(8,128)(2,1)S(1)}, bf16[256,256]{0,1:T(8,128)(2,1)S(1)}, u32[]{:S(2)}, u32[]{:S(2)}) %collective-permute-start.9) | collective-permute-done | bytes 131104 | tf_op jit(solution)/shard_map/ppermute | solution.py:12
  94.8 1.9 collective-permute-start.10
  97.1 4.0 %collective-permute-done.10 = bf16[256,256]{0,1:T(8,128)(2,1)S(1)} collective-permute-done((bf16[256,256]{0,1:T(8,128)(2,1)S(1)}, bf16[256,256]{0,1:T(8,128)(2,1)S(1)}, u32[]{:S(2)}, u32[]{:S(2)}) %collective-permute-start.10) | collective-permute-done | bytes 131104 | tf_op jit(solution)/shard_map/ppermute | solution.py:12
  101.2 1.9 collective-permute-start.11
  103.4 4.0 %collective-permute-done.11 = bf16[256,256]{0,1:T(8,128)(2,1)S(1)} collective-permute-done((bf16[256,256]{0,1:T(8,128)(2,1)S(1)}, bf16[256,256]{0,1:T(8,128)(2,1)S(1)}, u32[]{:S(2)}, u32[]{:S(2)}) %collective-permute-start.11) | collective-permute-done | bytes 131104 | tf_op jit(solution)/shard_map/ppermute | solution.py:12
  107.5 1.9 collective-permute-start.12
  109.7 4.0 %collective-permute-done.12 = bf16[256,256]{0,1:T(8,128)(2,1)S(1)} collective-permute-done((bf16[256,256]{0,1:T(8,128)(2,1)S(1)}, bf16[256,256]{0,1:T(8,128)(2,1)S(1)}, u32[]{:S(2)}, u32[]{:S(2)}) %collective-permute-start.12) | collective-permute-done | bytes 131104 | tf_op jit(solution)/shard_map/ppermute | solution.py:12
  113.8 2.1 %collective-permute-start.13 = (bf16[256,256]{0,1:T(8,128)(2,1)S(1)}, bf16[256,256]{0,1:T(8,128)(2,1)S(1)}, u32[]{:S(2)}, u32[]{:S(2)}) collective-permute-start(bf16[256,256]{0,1:T(8,128)(2,1)S(1)} %fusion.72), channel_id=1, source_target_pairs={{4,0},{8,4},{12,8},{16,12},{20,16},{24,20},{28,24},{32,28},{36,32}... | collective-permute-start | bytes 393224 | tf_op jit(solution)/shard_map/ppermute | solution.py:12
  116.3 3.9 %collective-permute-done.13 = bf16[256,256]{0,1:T(8,128)(2,1)S(1)} collective-permute-done((bf16[256,256]{0,1:T(8,128)(2,1)S(1)}, bf16[256,256]{0,1:T(8,128)(2,1)S(1)}, u32[]{:S(2)}, u32[]{:S(2)}) %collective-permute-start.13) | collective-permute-done | bytes 131104 | tf_op jit(solution)/shard_map/ppermute | solution.py:12
  120.2 0.7 maximum_add_fusion.6
  121.0 1.1 fusion.80
  122.4 0.6 copy-done.8
  123.3 0.7 copy-done.6
  124.4 0.8 copy-done.2
  125.4 0.4 fusion.24
  125.7 0.8 copy.139
  126.6 61.9 %all-gather.3.cloned.1.call-done = f32[1024,256]{0,1:T(8,128)} async-done(((f32[256,256]{0,1:T(8,128)}), f32[1024,256]{0,1:T(8,128)}) %all-gather.3.cloned.1.call-update) | async-done | bytes 1048592 | tf_op jit(solution)/shard_map/all_gather | solution.py:114
  188.5 1.7 reshape.387
  190.2 0.7 reduce_sum.169
  190.9 0.7 copy.141
  191.6 0.7 copy.140
  (84 shorter events, 12.2 us)
Async XLA Ops:
  7.2 16.9 %copy-start.12 = (bf16[256,512]{1,0:T(8,128)(2,1)S(1)}, bf16[256,512]{1,0:T(8,128)(2,1)}, u32[]{:S(2)}) copy-start(bf16[256,512]{1,0:T(8,128)(2,1)} %param.7) | copy-start | bytes 786436
  7.2 181.3 %all-gather.3.cloned.1.call-start = ((), (), s32[]{:S(2)}) async-start(), calls=%async_computation | async-start | bytes 1310720 | tf_op jit(solution)/shard_map/all_gather | solution.py:114
  8.1 22.1 %collective-permute-start = (bf16[256,256]{1,0:T(8,128)(2,1)S(1)}, bf16[256,256]{1,0:T(8,128)(2,1)S(1)}, u32[]{:S(2)}, u32[]{:S(2)}) collective-permute-start(bf16[256,256]{1,0:T(8,128)(2,1)S(1)} %pad_maximum_fusion), channel_id=1, source_target_pairs={{0,4},{4,8},{8,12},{12,16},{16,20},{20,24},{24,28},{28,32},{32,36}... | collective-permute-start | bytes 393224 | tf_op jit(solution)/shard_map/ppermute | solution.py:12
  13.6 0.7 copy-start.16
  22.0 1.2 copy-start.17
  24.1 1.0 copy-start.13
  25.0 4.6 %copy-start.15 = (s32[4,128]{1,0:T(4,128)S(1)}, s32[4,128]{1,0:T(4,128)}, u32[]{:S(2)}) copy-start(s32[4,128]{1,0:T(4,128)} %param.13) | copy-start | bytes 6148
  25.2 4.8 %copy-start.4 = (bf16[256,128]{1,0:T(8,128)(2,1)S(1)}, bf16[256,128]{1,0:T(8,128)(2,1)}, u32[]{:S(2)}) copy-start(bf16[256,128]{1,0:T(8,128)(2,1)} %param.8) | copy-start | bytes 196612
  30.3 4.9 %collective-permute-start.1 = (bf16[256,256]{1,0:T(8,128)(2,1)S(1)}, bf16[256,256]{1,0:T(8,128)(2,1)S(1)}, u32[]{:S(2)}, u32[]{:S(2)}) collective-permute-start(bf16[256,256]{1,0:T(8,128)(2,1)S(1)} %collective-permute-done), channel_id=1, source_target_pairs={{0,4},{4,8},{8,12},{12,16},{16,20},{20,24},{24,28},{28,32},{32,36}... | collective-permute-start | bytes 393224 | tf_op jit(solution)/shard_map/ppermute | solution.py:12
  35.2 33.5 %copy-start.5 = (bf16[256,256]{1,0:T(8,128)(2,1)}, bf16[256,256]{1,0:T(8,128)(2,1)S(1)}, u32[]{:S(2)}) copy-start(bf16[256,256]{1,0:T(8,128)(2,1)S(1)} %collective-permute-done.1) | copy-start | bytes 393220
  35.2 5.2 %collective-permute-start.2 = (bf16[256,256]{1,0:T(8,128)(2,1)S(1)}, bf16[256,256]{1,0:T(8,128)(2,1)S(1)}, u32[]{:S(2)}, u32[]{:S(2)}) collective-permute-start(bf16[256,256]{1,0:T(8,128)(2,1)S(1)} %collective-permute-done.1), channel_id=1, source_target_pairs={{0,4},{4,8},{8,12},{12,16},{16,20},{20,24},{24,28},{28,32},{32,36}... | collective-permute-start | bytes 393224 | tf_op jit(solution)/shard_map/ppermute | solution.py:12
  40.4 27.9 %copy-start.7 = (bf16[256,256]{1,0:T(8,128)(2,1)}, bf16[256,256]{1,0:T(8,128)(2,1)S(1)}, u32[]{:S(2)}) copy-start(bf16[256,256]{1,0:T(8,128)(2,1)S(1)} %collective-permute-done.2) | copy-start | bytes 393220
  40.4 6.3 %collective-permute-start.3 = (bf16[256,256]{1,0:T(8,128)(2,1)S(1)}, bf16[256,256]{1,0:T(8,128)(2,1)S(1)}, u32[]{:S(2)}, u32[]{:S(2)}) collective-permute-start(bf16[256,256]{1,0:T(8,128)(2,1)S(1)} %collective-permute-done.2), channel_id=1, source_target_pairs={{0,4},{4,8},{8,12},{12,16},{16,20},{20,24},{24,28},{28,32},{32,36}... | collective-permute-start | bytes 393224 | tf_op jit(solution)/shard_map/ppermute | solution.py:12
  46.7 21.3 %copy-start.9 = (bf16[256,256]{1,0:T(8,128)(2,1)}, bf16[256,256]{1,0:T(8,128)(2,1)S(1)}, u32[]{:S(2)}) copy-start(bf16[256,256]{1,0:T(8,128)(2,1)S(1)} %collective-permute-done.3) | copy-start | bytes 393220
  46.7 6.3 %collective-permute-start.4 = (bf16[256,256]{1,0:T(8,128)(2,1)S(1)}, bf16[256,256]{1,0:T(8,128)(2,1)S(1)}, u32[]{:S(2)}, u32[]{:S(2)}) collective-permute-start(bf16[256,256]{1,0:T(8,128)(2,1)S(1)} %collective-permute-done.3), channel_id=1, source_target_pairs={{0,4},{4,8},{8,12},{12,16},{16,20},{20,24},{24,28},{28,32},{32,36}... | collective-permute-start | bytes 393224 | tf_op jit(solution)/shard_map/ppermute | solution.py:12
  53.0 14.7 %copy-start.11 = (bf16[256,256]{1,0:T(8,128)(2,1)}, bf16[256,256]{1,0:T(8,128)(2,1)S(1)}, u32[]{:S(2)}) copy-start(bf16[256,256]{1,0:T(8,128)(2,1)S(1)} %collective-permute-done.4) | copy-start | bytes 393220
  53.0 6.3 %collective-permute-start.5 = (bf16[256,256]{1,0:T(8,128)(2,1)S(1)}, bf16[256,256]{1,0:T(8,128)(2,1)S(1)}, u32[]{:S(2)}, u32[]{:S(2)}) collective-permute-start(bf16[256,256]{1,0:T(8,128)(2,1)S(1)} %collective-permute-done.4), channel_id=1, source_target_pairs={{0,4},{4,8},{8,12},{12,16},{16,20},{20,24},{24,28},{28,32},{32,36}... | collective-permute-start | bytes 393224 | tf_op jit(solution)/shard_map/ppermute | solution.py:12
  59.2 6.3 %collective-permute-start.6 = (bf16[256,256]{1,0:T(8,128)(2,1)S(1)}, bf16[256,256]{1,0:T(8,128)(2,1)S(1)}, u32[]{:S(2)}, u32[]{:S(2)}) collective-permute-start(bf16[256,256]{1,0:T(8,128)(2,1)S(1)} %collective-permute-done.5), channel_id=1, source_target_pairs={{0,4},{4,8},{8,12},{12,16},{16,20},{20,24},{24,28},{28,32},{32,36}... | collective-permute-start | bytes 393224 | tf_op jit(solution)/shard_map/ppermute | solution.py:12
  65.8 0.8 copy-start.14
  71.5 2.0 %copy-start = (bf16[4,256,256]{1,2,0:T(8,128)(2,1)}, bf16[4,256,256]{1,2,0:T(8,128)(2,1)S(1)}, u32[]{:S(2)}) copy-start(bf16[4,256,256]{1,2,0:T(8,128)(2,1)S(1)} %get-tuple-element.52) | copy-start | bytes 1572868
  75.2 7.0 %collective-permute-start.7 = (bf16[256,256]{0,1:T(8,128)(2,1)S(1)}, bf16[256,256]{0,1:T(8,128)(2,1)S(1)}, u32[]{:S(2)}, u32[]{:S(2)}) collective-permute-start(bf16[256,256]{0,1:T(8,128)(2,1)S(1)} %pad_maximum_fusion.1), channel_id=1, source_target_pairs={{4,0},{8,4},{12,8},{16,12},{20,16},{24,20},{28,24},{32,28},{36,32}... | collective-permute-start | bytes 393224 | tf_op jit(solution)/shard_map/ppermute | solution.py:12
  82.2 6.3 %collective-permute-start.8 = (bf16[256,256]{0,1:T(8,128)(2,1)S(1)}, bf16[256,256]{0,1:T(8,128)(2,1)S(1)}, u32[]{:S(2)}, u32[]{:S(2)}) collective-permute-start(bf16[256,256]{0,1:T(8,128)(2,1)S(1)} %fusion.67), channel_id=1, source_target_pairs={{4,0},{8,4},{12,8},{16,12},{20,16},{24,20},{28,24},{32,28},{36,32}... | collective-permute-start | bytes 393224 | tf_op jit(solution)/shard_map/ppermute | solution.py:12
  88.5 6.3 %collective-permute-start.9 = (bf16[256,256]{0,1:T(8,128)(2,1)S(1)}, bf16[256,256]{0,1:T(8,128)(2,1)S(1)}, u32[]{:S(2)}, u32[]{:S(2)}) collective-permute-start(bf16[256,256]{0,1:T(8,128)(2,1)S(1)} %fusion.68), channel_id=1, source_target_pairs={{4,0},{8,4},{12,8},{16,12},{20,16},{24,20},{28,24},{32,28},{36,32}... | collective-permute-start | bytes 393224 | tf_op jit(solution)/shard_map/ppermute | solution.py:12
  94.8 6.3 %collective-permute-start.10 = (bf16[256,256]{0,1:T(8,128)(2,1)S(1)}, bf16[256,256]{0,1:T(8,128)(2,1)S(1)}, u32[]{:S(2)}, u32[]{:S(2)}) collective-permute-start(bf16[256,256]{0,1:T(8,128)(2,1)S(1)} %fusion.69), channel_id=1, source_target_pairs={{4,0},{8,4},{12,8},{16,12},{20,16},{24,20},{28,24},{32,28},{36,32}... | collective-permute-start | bytes 393224 | tf_op jit(solution)/shard_map/ppermute | solution.py:12
  101.2 6.3 %collective-permute-start.11 = (bf16[256,256]{0,1:T(8,128)(2,1)S(1)}, bf16[256,256]{0,1:T(8,128)(2,1)S(1)}, u32[]{:S(2)}, u32[]{:S(2)}) collective-permute-start(bf16[256,256]{0,1:T(8,128)(2,1)S(1)} %fusion.70), channel_id=1, source_target_pairs={{4,0},{8,4},{12,8},{16,12},{20,16},{24,20},{28,24},{32,28},{36,32}... | collective-permute-start | bytes 393224 | tf_op jit(solution)/shard_map/ppermute | solution.py:12
  107.5 6.3 %collective-permute-start.12 = (bf16[256,256]{0,1:T(8,128)(2,1)S(1)}, bf16[256,256]{0,1:T(8,128)(2,1)S(1)}, u32[]{:S(2)}, u32[]{:S(2)}) collective-permute-start(bf16[256,256]{0,1:T(8,128)(2,1)S(1)} %fusion.71), channel_id=1, source_target_pairs={{4,0},{8,4},{12,8},{16,12},{20,16},{24,20},{28,24},{32,28},{36,32}... | collective-permute-start | bytes 393224 | tf_op jit(solution)/shard_map/ppermute | solution.py:12
  113.8 6.4 %collective-permute-start.13 = (bf16[256,256]{0,1:T(8,128)(2,1)S(1)}, bf16[256,256]{0,1:T(8,128)(2,1)S(1)}, u32[]{:S(2)}, u32[]{:S(2)}) collective-permute-start(bf16[256,256]{0,1:T(8,128)(2,1)S(1)} %fusion.72), channel_id=1, source_target_pairs={{4,0},{8,4},{12,8},{16,12},{20,16},{24,20},{28,24},{32,28},{36,32}... | collective-permute-start | bytes 393224 | tf_op jit(solution)/shard_map/ppermute | solution.py:12
  116.2 4.7 %copy-start.1 = (bf16[4,256,256]{1,2,0:T(8,128)(2,1)S(1)}, bf16[4,256,256]{1,2,0:T(8,128)(2,1)}, u32[]{:S(2)}) copy-start(bf16[4,256,256]{1,2,0:T(8,128)(2,1)} %copy-done) | copy-start | bytes 1572868
  121.0 1.1 copy-start.10
  122.1 0.9 copy-start.8
  123.0 0.9 copy-start.6
  124.2 1.0 copy-start.2
  124.2 1.2 copy-start.3
Sparse Core Ops, SparseCore 0:
  121.1 67.3 all-gather.2
